TPU v7x, 512 devices: a whole 4x4x16 slice. The times are simulated.
512 devices in a mesh: gy: 32 (over x, y, core), gz: 16 (over z).
Axes of the slice: x: 4, y: 4, z: 16, core: 2. Of those that a mesh axis runs over, the one named last changes fastest.
Arguments:
- volume: bfloat16 [64, 128, 64, 256], P(None, 'gy', 'gz'), may hold values from -2500 to 2500
- down_weight: bfloat16 [128, 64, 2, 2, 2], replicated, may hold values from -0.25 to 0.25
- conv_one: bfloat16 [3, 3, 128, 384], replicated, may hold values from -0.109375 to 0.109375
- conv_two: bfloat16 [3, 3, 128, 384], replicated, may hold values from -0.109375 to 0.109375
- norm_gain: float32 [3, 128], replicated, may hold values from 0.1 to 1.9
- norm_shift: float32 [3, 128], replicated, may hold values from -2.5 to 2.5
Outputs:
- features: bfloat16 [128, 64, 32, 128], P(None, 'gy', 'gz')
All inputs are finite; a program needn't handle non-finite values.
Results may differ from a plain program's by a relative error of at most 0.0065.
Values may be sent and summed in bfloat16 or wider, within the bound.
No kernel may reach another device: no remote copies, remote signals or barrier semaphores. Data moves between devices by JAX's collectives and lax.ppermute only.
A program may use at most 64 MiB of HBM per device.

v0:
```python
import jax
import jax.numpy as jnp
from jax import lax
from jax.sharding import PartitionSpec as P


def padded_2(value, sides, width):
    for axis, dim in sides:
        count, length = (lax.axis_size(axis), value.shape[dim])
        up = [(i, (i + 1) % count) for i in range(count - 1)]
        down = [(j, i) for i, j in up]
        last = lax.slice_in_dim(value, length - width, length, axis=dim)
        leading = lax.slice_in_dim(value, 0, width, axis=dim)
        before = lax.ppermute(last, axis, up)
        after = lax.ppermute(leading, axis, down)
        value = jnp.concatenate([before, value, after], axis=dim)
    return value


def leaky(value):
    return jnp.where(value >= 0.0, value, 0.01 * value)


def moments(inner):
    count = float(
        inner.shape[1] * inner.shape[2] * inner.shape[3] * lax.axis_size("gy") * lax.axis_size("gz")
    )
    total = lax.psum(jnp.sum(inner, axis=(1, 2, 3)), ("gy", "gz"))
    mean = total / count
    centered = inner - mean[:, None, None, None]
    spread = lax.psum(jnp.sum(centered * centered, axis=(1, 2, 3)), ("gy", "gz")) / count
    return (mean, spread)


def normalize(value, inner, gain, shift):
    mean, spread = moments(inner)
    scaled = (value - mean[:, None, None, None]) / jnp.sqrt(spread + 1e-05)[:, None, None, None]
    return leaky(scaled * gain[:, None, None, None] + shift[:, None, None, None])


def strided(volume, down_weight):
    blocks = volume.reshape(
        volume.shape[0], volume.shape[1] // 2, 2, volume.shape[2] // 2, 2, volume.shape[3] // 2, 2
    )
    return jnp.einsum(
        "oiabc,iyazbxc->oyzx", down_weight, blocks, preferred_element_type=jnp.float32
    )


def convolve(padded, conv_weight, rows, depth):
    length = padded.shape[3]
    widened = jnp.pad(padded, ((0, 0), (0, 0), (0, 0), (1, 1)))
    stacked = jnp.concatenate(
        [widened[:, :, :, offset : offset + length] for offset in range(3)], axis=0
    )
    total = jnp.zeros((conv_weight.shape[2], rows, depth, length), jnp.float32)
    for row_tap in range(3):
        for depth_tap in range(3):
            piece = stacked[:, row_tap : row_tap + rows, depth_tap : depth_tap + depth, :]
            total = total + jnp.einsum(
                "ok,kyzx->oyzx",
                conv_weight[row_tap, depth_tap],
                piece,
                preferred_element_type=jnp.float32,
            )
    return total


def faces(field):
    return padded_2(field, (("gy", 1), ("gz", 2)), 1)


def on_device(volume, down_weight, conv_one, conv_two, norm_gain, norm_shift):
    coarse = strided(volume, down_weight)
    rows = coarse.shape[1]
    depth = coarse.shape[2]
    first = normalize(coarse, coarse, norm_gain[0], norm_shift[0]).astype(jnp.bfloat16)
    middle = convolve(faces(first), conv_one, rows, depth)
    second = normalize(middle, middle, norm_gain[1], norm_shift[1]).astype(jnp.bfloat16)
    last = convolve(faces(second), conv_two, rows, depth)
    return normalize(last, last, norm_gain[2], norm_shift[2]).astype(jnp.bfloat16)


def solution(mesh):
    return jax.shard_map(
        on_device,
        mesh=mesh,
        in_specs=(P(None, "gy", "gz", None), P(), P(), P(), P(), P()),
        out_specs=P(None, "gy", "gz", None),
        check_vma=False,
    )
```

profile of v0, /device:TPU:1, one launch (start us, length us, event | category | flops | bytes accessed | tf_op | source)
XLA Modules:
  0.0 662.0 jit_solution(10334304953308035063)
XLA Ops:
  0.0 1.7 copy.10
  2.1 111.0 %psum.42 = f32[128]{0:T(128)S(1)} all-reduce(f32[128]{0:T(128)S(1)} %get-tuple-element.23), channel_id=1, replica_groups=mesh['gy'=32,'gz'=16] {'gy','gz'}, use_global_device_ids=true, to_apply=%region_1.0 | all-reduce | flops 128 | bytes 1024 | tf_op jit(solution)/shard_map/psum | solution.py:28
  113.2 98.2 %psum.43 = f32[128]{0:T(128)S(1)} all-reduce(f32[128]{0:T(128)S(1)} %multiply_reduce_fusion.2), channel_id=1, replica_groups=mesh['gy'=32,'gz'=16] {'gy','gz'}, use_global_device_ids=true, to_apply=%region_3.0 | all-reduce | flops 128 | bytes 1024 | tf_op jit(solution)/shard_map/psum | solution.py:31
  211.6 2.9 collective-permute-start
  214.5 1.9 collective-permute-start.1
  216.4 3.6 collective-permute-done.1
  220.1 3.7 collective-permute-start.2
  223.8 1.3 collective-permute-start.3
  225.1 0.6 collective-permute-done.2
  225.7 3.8 collective-permute-done.3
  230.2 0.9 copy-done
  233.6 102.8 %psum.44 = f32[128]{0:T(128)S(1)} all-reduce(f32[128]{0:T(128)S(1)} %get-tuple-element.25), channel_id=1, replica_groups=mesh['gy'=32,'gz'=16] {'gy','gz'}, use_global_device_ids=true, to_apply=%region_5.6 | all-reduce | flops 128 | bytes 1024 | tf_op jit(solution)/shard_map/psum | solution.py:28
  336.5 99.5 %psum.45 = f32[128]{0:T(128)S(1)} all-reduce(f32[128]{0:T(128)S(1)} %multiply_reduce_fusion.1), channel_id=1, replica_groups=mesh['gy'=32,'gz'=16] {'gy','gz'}, use_global_device_ids=true, to_apply=%region_7.8 | all-reduce | flops 128 | bytes 1024 | tf_op jit(solution)/shard_map/psum | solution.py:31
  436.1 3.4 collective-permute-start.4
  439.6 1.9 collective-permute-start.5
  441.5 3.6 collective-permute-done.5
  445.2 3.7 collective-permute-start.6
  448.9 1.3 collective-permute-start.7
  450.2 0.6 collective-permute-done.6
  450.8 3.8 collective-permute-done.7
  455.3 0.9 copy-done.1
  458.7 102.7 %psum.46 = f32[128]{0:T(128)S(1)} all-reduce(f32[128]{0:T(128)S(1)} %get-tuple-element.27), channel_id=1, replica_groups=mesh['gy'=32,'gz'=16] {'gy','gz'}, use_global_device_ids=true, to_apply=%region_9.10 | all-reduce | flops 128 | bytes 1024 | tf_op jit(solution)/shard_map/psum | solution.py:28
  561.5 99.5 %psum.47 = f32[128]{0:T(128)S(1)} all-reduce(f32[128]{0:T(128)S(1)} %multiply_reduce_fusion), channel_id=1, replica_groups=mesh['gy'=32,'gz'=16] {'gy','gz'}, use_global_device_ids=true, to_apply=%region_11.12 | all-reduce | flops 128 | bytes 1024 | tf_op jit(solution)/shard_map/psum | solution.py:31
  661.2 0.8 copy.13
  (54 shorter events, 7.3 us)
Async XLA Ops:
  0.0 1.7 copy-start.4
  0.0 211.4 %copy-start.2 = (f32[3,128]{1,0:T(4,128)S(1)}, f32[3,128]{1,0:T(4,128)}, u32[]{:S(2)}) copy-start(f32[3,128]{1,0:T(4,128)} %param.11) | copy-start | bytes 4612
  0.0 211.4 %copy-start.3 = (f32[3,128]{1,0:T(4,128)S(1)}, f32[3,128]{1,0:T(4,128)}, u32[]{:S(2)}) copy-start(f32[3,128]{1,0:T(4,128)} %param.10) | copy-start | bytes 4612
  211.6 4.8 collective-permute-start
  214.5 5.6 collective-permute-start.1
  220.1 5.6 collective-permute-start.2
  223.8 5.7 collective-permute-start.3
  230.0 1.2 copy-start
  436.1 5.4 collective-permute-start.4
  439.6 5.6 collective-permute-start.5
  445.2 5.6 collective-permute-start.6
  448.9 5.7 collective-permute-start.7
  455.1 1.2 copy-start.1
where the time goes:
time: 663 us; the launch traced here: 662 us
  blocking collectives  614 us (93%)
  starting transfers between devices  20.1 us (3%)
  waiting for transfers between devices  16.1 us (2%)
    psum x3, blocking collectives, moments(): total = lax.psum(jnp.sum(inner, axis=(1, 2, 3)), ('gy', 'gz'))  317 us
    psum x3, blocking collectives, moments(): lax.psum(jnp.sum(centered * centered, axis=(1, 2, 3)), ('gy', 'gz')) / count  297 us
    ppermute x4, waiting for transfers between devices, padded_2(): after = lax.ppermute(leading, axis, down)  14.9 us
    ppermute x4, starting transfers between devices, padded_2(): before = lax.ppermute(last, axis, up)  13.7 us
  transfers between devices with their start and end apart: 8, of which 6 were waited for; matrix products, arithmetic and copies ran while one was open for 0% of the time, Pallas kernels for 0%

commit v1 on v0

--- a/solution.py
+++ b/solution.py
@@ -25,7 +25,7 @@
     count = float(
         inner.shape[1] * inner.shape[2] * inner.shape[3] * lax.axis_size("gy") * lax.axis_size("gz")
     )
-    total = lax.psum(jnp.sum(inner, axis=(1, 2, 3)), ("gy", "gz"))
+    total = lax.psum(lax.psum(jnp.sum(inner, axis=(1, 2, 3)), "gz"), "gy")
     mean = total / count
     centered = inner - mean[:, None, None, None]
     spread = lax.psum(jnp.sum(centered * centered, axis=(1, 2, 3)), ("gy", "gz")) / count

time: 663 us -> 624 us (0.941)
  blocking collectives: 614 us -> 577 us
    psum x3 -> x6, blocking collectives: 317 us -> 280 us  [moments(): total = lax.psum(lax.psum(jnp.sum(inner, axis=(1, 2, 3)), 'gz'), 'gy')]
where the time goes in v1:
time: 624 us; the launch traced here: 623 us
  blocking collectives  577 us (92%)
  starting transfers between devices  18.6 us (3%)
  waiting for transfers between devices  15.6 us (2%)
    psum x3, blocking collectives, moments(): lax.psum(jnp.sum(centered * centered, axis=(1, 2, 3)), ('gy', 'gz')) / count  296 us
    psum x6, blocking collectives, moments(): total = lax.psum(lax.psum(jnp.sum(inner, axis=(1, 2, 3)), 'gz'), 'gy')  280 us
    ppermute x4, waiting for transfers between devices, padded_2(): after = lax.ppermute(leading, axis, down)  14.3 us
  transfers between devices with their start and end apart: 8, of which 6 were waited for; matrix products, arithmetic and copies ran while one was open for 0% of the time, Pallas kernels for 0%

profile of v1, /device:TPU:1, one launch (start us, length us, event | category | flops | bytes accessed | tf_op | source)
XLA Modules:
  0.0 622.8 jit_solution(9052674596972739174)
XLA Ops:
  0.0 1.7 copy.10
  2.1 30.3 %psum.63 = f32[128]{0:T(128)S(1)} all-reduce(f32[128]{0:T(128)S(1)} %get-tuple-element.23), channel_id=1, replica_groups=mesh['gy'=32,'gz'=16] {'gz'}, use_global_device_ids=true, to_apply=%region_1.0 | all-reduce | flops 128 | bytes 1024 | tf_op jit(solution)/shard_map/psum | solution.py:28
  32.4 69.9 %psum.64 = f32[128]{0:T(128)S(1)} all-reduce(f32[128]{0:T(128)S(1)} %psum.63), channel_id=1, replica_groups=mesh['gy'=32,'gz'=16] {'gy'}, use_global_device_ids=true, to_apply=%region_2.0 | all-reduce | flops 128 | bytes 1024 | tf_op jit(solution)/shard_map/psum | solution.py:28
  102.4 98.7 %psum.65 = f32[128]{0:T(128)S(1)} all-reduce(f32[128]{0:T(128)S(1)} %multiply_reduce_fusion.2), channel_id=1, replica_groups=mesh['gy'=32,'gz'=16] {'gy','gz'}, use_global_device_ids=true, to_apply=%region_4.0 | all-reduce | flops 128 | bytes 1024 | tf_op jit(solution)/shard_map/psum | solution.py:31
  201.3 1.9 collective-permute-start
  203.2 2.4 collective-permute-start.1
  205.7 3.2 collective-permute-done.1
  208.9 3.7 collective-permute-start.2
  212.6 1.3 collective-permute-start.3
  214.5 4.0 collective-permute-done.3
  219.2 0.9 copy-done
  222.6 21.4 %psum.66 = f32[128]{0:T(128)S(1)} all-reduce(f32[128]{0:T(128)S(1)} %get-tuple-element.25), channel_id=1, replica_groups=mesh['gy'=32,'gz'=16] {'gz'}, use_global_device_ids=true, to_apply=%region_6.7 | all-reduce | flops 128 | bytes 1024 | tf_op jit(solution)/shard_map/psum | solution.py:28
  244.0 68.2 %psum.67 = f32[128]{0:T(128)S(1)} all-reduce(f32[128]{0:T(128)S(1)} %psum.66), channel_id=1, replica_groups=mesh['gy'=32,'gz'=16] {'gy'}, use_global_device_ids=true, to_apply=%region_7.8 | all-reduce | flops 128 | bytes 1024 | tf_op jit(solution)/shard_map/psum | solution.py:28
  312.3 98.8 %psum.68 = f32[128]{0:T(128)S(1)} all-reduce(f32[128]{0:T(128)S(1)} %multiply_reduce_fusion.1), channel_id=1, replica_groups=mesh['gy'=32,'gz'=16] {'gy','gz'}, use_global_device_ids=true, to_apply=%region_9.10 | all-reduce | flops 128 | bytes 1024 | tf_op jit(solution)/shard_map/psum | solution.py:31
  411.2 2.1 collective-permute-start.4
  413.3 2.2 collective-permute-start.5
  415.6 3.3 collective-permute-done.5
  419.0 3.7 collective-permute-start.6
  422.7 1.3 collective-permute-start.7
  424.6 3.8 collective-permute-done.7
  429.1 0.9 copy-done.1
  432.5 22.6 %psum.69 = f32[128]{0:T(128)S(1)} all-reduce(f32[128]{0:T(128)S(1)} %get-tuple-element.27), channel_id=1, replica_groups=mesh['gy'=32,'gz'=16] {'gz'}, use_global_device_ids=true, to_apply=%region_11.12 | all-reduce | flops 128 | bytes 1024 | tf_op jit(solution)/shard_map/psum | solution.py:28
  455.1 67.9 %psum.70 = f32[128]{0:T(128)S(1)} all-reduce(f32[128]{0:T(128)S(1)} %psum.69), channel_id=1, replica_groups=mesh['gy'=32,'gz'=16] {'gy'}, use_global_device_ids=true, to_apply=%region_12.13 | all-reduce | flops 128 | bytes 1024 | tf_op jit(solution)/shard_map/psum | solution.py:28
  523.2 98.8 %psum.71 = f32[128]{0:T(128)S(1)} all-reduce(f32[128]{0:T(128)S(1)} %multiply_reduce_fusion), channel_id=1, replica_groups=mesh['gy'=32,'gz'=16] {'gy','gz'}, use_global_device_ids=true, to_apply=%region_14.15 | all-reduce | flops 128 | bytes 1024 | tf_op jit(solution)/shard_map/psum | solution.py:31
  (57 shorter events, 9.3 us)
Async XLA Ops:
  0.0 1.7 copy-start.4
  0.0 201.2 %copy-start.2 = (f32[3,128]{1,0:T(4,128)S(1)}, f32[3,128]{1,0:T(4,128)}, u32[]{:S(2)}) copy-start(f32[3,128]{1,0:T(4,128)} %param.11) | copy-start | bytes 4612
  0.0 201.2 %copy-start.3 = (f32[3,128]{1,0:T(4,128)S(1)}, f32[3,128]{1,0:T(4,128)}, u32[]{:S(2)}) copy-start(f32[3,128]{1,0:T(4,128)} %param.10) | copy-start | bytes 4612
  201.3 4.3 collective-permute-start
  203.2 5.6 collective-permute-start.1
  208.9 5.6 collective-permute-start.2
  212.6 5.9 collective-permute-start.3
  218.9 1.2 copy-start
  411.2 4.3 collective-permute-start.4
  413.3 5.6 collective-permute-start.5
  419.0 5.6 collective-permute-start.6
  422.7 5.8 collective-permute-start.7
  428.9 1.2 copy-start.1
